TPU v7x, 128 devices: a whole 4x4x4 slice. The times are simulated.
128 devices in a mesh: igrp: 8 (over x, core), jgrp: 16 (over y, z).
Axes of the slice: x: 4, y: 4, z: 4, core: 2. Of those that a mesh axis runs over, the one named last changes fastest.
Arguments:
- t_start: bfloat16 [64, 64, 256, 256], P('igrp', 'jgrp'), may hold values from -2.390625 to 2.390625
- integrals: bfloat16 [64, 64, 256, 256], P('igrp', 'jgrp'), may hold values from -6 to 6
- weights: bfloat16 [64, 8, 256, 256], P('igrp'), may hold values from -0.125 to 0.125
- neighbours: int32 [64, 8], replicated, may hold values from 0 to 63, as said below
- eps_occ: float32 [64], replicated, may hold values from -2 to -0.5
- eps_vir: float32 [256], replicated, may hold values from 0.2 to 4
Outputs:
- amplitudes: float32 [64, 64, 256, 256], P('igrp', 'jgrp')
Inputs may be any that keep to these rules, and one draw needn't show every extreme that they name: `neighbours`: the entries of a row are distinct. For every block of 8 consecutive rows starting at a multiple of 8, and every block of 8 consecutive orbitals starting at a multiple of 8, exactly 2 distinct orbitals of that block appear in those rows.
All inputs are finite; a program needn't handle non-finite values.
Results may differ from a plain program's by a relative error of at most 0.0018.
Values may be sent and summed in bfloat16 or wider, within the bound.
A program may use at most 128 MiB of HBM per device.

v0:
```python
import jax
import jax.numpy as jnp
from jax import lax
from jax.sharding import PartitionSpec as P

NNB = 8
CAP = 2
ITERS = 2


def first_true(flags, capacity):
    counted = flags.shape[1]
    ranking = jnp.cumsum(flags.astype(jnp.int32), axis=1) - 1
    offsets = jnp.arange(counted, dtype=jnp.int32)
    hits = flags[:, :, None] & (
        ranking[:, :, None] == jnp.arange(capacity, dtype=jnp.int32)[None, None, :]
    )
    return jnp.sum(offsets[None, :, None] * hits.astype(jnp.int32), axis=1)


def transposed(cycle_term):
    section_one = lax.all_to_all(cycle_term, "jgrp", split_axis=2, concat_axis=1, tiled=True)
    section_two = lax.all_to_all(section_one, "igrp", split_axis=1, concat_axis=0, tiled=True)
    section_three = lax.all_to_all(section_two, "jgrp", split_axis=0, concat_axis=2, tiled=True)
    return section_three.transpose(1, 0, 3, 2)


def body(t_start, integrals, weights, neighbours, eps_occ, eps_vir):
    row_count = weights.shape[0]
    col_count = t_start.shape[1]
    capacity = CAP
    igroups = lax.axis_size("igrp")
    my_igrp = lax.axis_index("igrp")
    my_jgrp = lax.axis_index("jgrp")
    grouped = neighbours.reshape(igroups, row_count * NNB)
    own_orbitals = my_igrp * row_count + jnp.arange(row_count, dtype=jnp.int32)
    wanted = jnp.any(grouped[:, :, None] == own_orbitals[None, None, :], axis=1)
    send_choice = first_true(wanted, capacity).reshape(-1)
    my_rows = lax.dynamic_slice_in_dim(neighbours, my_igrp * row_count, row_count, 0)
    flat_list = my_rows.reshape(-1)
    all_blocks = jnp.arange(igroups * row_count, dtype=jnp.int32).reshape(igroups, row_count)
    needed = jnp.any(flat_list[None, None, :] == all_blocks[:, :, None], axis=2)
    recv_orbitals = (
        first_true(needed, capacity) + (jnp.arange(igroups, dtype=jnp.int32) * row_count)[:, None]
    ).reshape(-1)
    slot_index = jnp.sum(
        jnp.arange(igroups * capacity, dtype=jnp.int32)[None, None, :]
        * (my_rows[:, :, None] == recv_orbitals[None, None, :]).astype(jnp.int32),
        axis=2,
    )
    occ_rows = lax.dynamic_slice_in_dim(eps_occ, my_igrp * row_count, row_count, 0)
    occ_cols = lax.dynamic_slice_in_dim(eps_occ, my_jgrp * col_count, col_count, 0)
    denominator = (
        eps_vir[None, None, :, None]
        + eps_vir[None, None, None, :]
        - occ_rows[:, None, None, None]
        - occ_cols[None, :, None, None]
    )
    current = t_start
    updated = t_start.astype(jnp.float32)
    for sweep in range(ITERS):
        outgoing = jnp.take(current, send_choice, axis=0)
        received = lax.all_to_all(outgoing, "igrp", split_axis=0, concat_axis=0, tiled=True)

        def per_row(state_in, inputs):
            weight_rows, slot_rows = inputs
            picked = jnp.take(received, slot_rows, axis=0)
            product = jnp.einsum(
                "mac,mjcb->jab", weight_rows, picked, preferred_element_type=jnp.float32
            )
            return (state_in, product.astype(jnp.bfloat16))

        _, cycle_term = lax.scan(per_row, jnp.zeros((), jnp.int32), (weights, slot_index))
        flipped = transposed(cycle_term)
        updated = (
            integrals.astype(jnp.float32)
            + cycle_term.astype(jnp.float32)
            + flipped.astype(jnp.float32)
        ) / denominator
        current = updated.astype(jnp.bfloat16)
    return updated


def solution(mesh):
    placed = (
        P("igrp", "jgrp", None, None),
        P("igrp", "jgrp", None, None),
        P("igrp", None, None, None),
        P(),
        P(),
        P(),
    )
    return jax.shard_map(
        body, mesh=mesh, in_specs=placed, out_specs=P("igrp", "jgrp", None, None), check_vma=False
    )
```

profile of v0, /device:TPU:0, one launch (start us, length us, event | category | flops | bytes accessed | tf_op | source)
XLA Modules:
  0.0 837.1 jit_solution(9905293060247468984)
XLA Ops:
  1.7 7.1 gather_fusion.2
  8.7 7.6 broadcast_select_fusion.1
  22.8 93.2 %all-to-all-done = bf16[16,4,256,256]{3,2,1,0:T(8,128)(2,1)} async-done(((bf16[16,4,256,256]{3,2,1,0:T(8,128)(2,1)}), bf16[16,4,256,256]{3,2,1,0:T(8,128)(2,1)}, u32[]{:S(2)}, u32[]{:S(2)}) %all-to-all-start) | async-done | bytes 8388640 | tf_op jit(solution)/shard_map/all_to_all | solution.py:63
  118.5 88.0 %while.20 = (s32[]{:T(128)}, bf16[8,4,256,256]{2,3,1,0:T(8,128)(2,1)}, s32[8,8]{1,0:T(8,128)S(1)}, bf16[16,4,256,256]{3,2,1,0:T(8,128)(2,1)}, bf16[8,8,256,256]{3,2,1,0:T(8,128)(2,1)}, /*index=5*/s32[]{:T(128)}) while((s32[]{:T(128)}, bf16[8,4,256,256]{2,3,1,0:T(8,128)(2,1)}, s32[8,8]{1,0:T(8,128)S(1)}, bf16[16,4,256,256]{3,2,1,0:T(8,128)(2,1)}, ...), condition=%wide.region_8.11_spmd, body=%wide.region_7.10_spmd.sunk | while | flops 1076102144 | bytes 14161113 | solution.py:73
  129.5 6.2 gather_fusion
  140.6 6.2 gather_fusion
  151.6 6.2 gather_fusion
  173.6 6.2 gather_fusion
  206.5 7.8 copy.84
  214.3 58.7 %all_to_all.100 = bf16[8,4,256,256]{3,1,0,2:T(4,128)(2,1)S(1)} all-to-all(bf16[8,4,256,256]{3,1,0,2:T(4,128)(2,1)} %copy.84), channel_id=1, replica_groups=mesh['igrp'=8,'jgrp'=16] {'jgrp'}, dimensions={2} | all-to-all | bytes 8388608 | tf_op jit(solution)/shard_map/all_to_all | solution.py:22
  276.7 52.2 %all_to_all.101 = bf16[8,64,16,256]{3,2,0,1:T(8,128)(2,1)S(1)} all-to-all(bf16[8,64,16,256]{3,2,0,1:T(8,128)(2,1)S(1)} %copy.87), channel_id=1, replica_groups=mesh['igrp'=8,'jgrp'=16] {'igrp'}, dimensions={1} | all-to-all | bytes 8388608 | tf_op jit(solution)/shard_map/all_to_all | solution.py:23
  336.5 6.2 copy.77
  343.1 57.6 %all-to-all-done.3 = bf16[64,8,16,256]{3,2,1,0:T(8,128)(2,1)} async-done(((bf16[64,8,16,256]{3,2,1,0:T(8,128)(2,1)}), bf16[64,8,16,256]{3,2,1,0:T(8,128)(2,1)}, u32[]{:S(2)}, u32[]{:S(2)}) %all-to-all-start.3) | async-done | bytes 4194336 | tf_op jit(solution)/shard_map/all_to_all | solution.py:24
  400.7 6.8 convert_bitcast_fusion.1
  417.7 7.0 gather_fusion.3
  424.7 7.6 broadcast_select_fusion
  432.4 100.3 %all_to_all.102 = bf16[16,4,256,256]{2,3,1,0:T(8,128)(2,1)} all-to-all(bf16[16,4,256,256]{2,3,1,0:T(8,128)(2,1)} %broadcast_select_fusion), channel_id=1, replica_groups=mesh['igrp'=8,'jgrp'=16] {'igrp'}, dimensions={0} | all-to-all | bytes 16777216 | tf_op jit(solution)/shard_map/all_to_all | solution.py:63
  532.7 12.2 %copy.91 = bf16[16,4,256,256]{3,2,1,0:T(8,128)(2,1)} copy(bf16[16,4,256,256]{2,3,1,0:T(8,128)(2,1)} %all_to_all.102) | data formatting | bytes 16777216 | tf_op jit(solution)/shard_map/while | solution.py:73
  547.3 87.7 %while.21 = (s32[]{:T(128)}, bf16[8,4,256,256]{2,3,1,0:T(8,128)(2,1)}, s32[8,8]{1,0:T(8,128)S(1)}, bf16[16,4,256,256]{3,2,1,0:T(8,128)(2,1)}, bf16[8,8,256,256]{3,2,1,0:T(8,128)(2,1)}, /*index=5*/s32[]{:T(128)}) while((s32[]{:T(128)}, bf16[8,4,256,256]{2,3,1,0:T(8,128)(2,1)}, s32[8,8]{1,0:T(8,128)S(1)}, ...), condition=%wide.region_10.13_spmd, body=%wide.region_9.12_spmd.sunk | while | flops 1076102144 | bytes 14161113 | solution.py:73
  635.0 7.8 copy.93
  642.9 58.3 %all_to_all.103 = bf16[8,4,256,256]{3,1,0,2:T(4,128)(2,1)S(1)} all-to-all(bf16[8,4,256,256]{3,1,0,2:T(4,128)(2,1)} %copy.93), channel_id=1, replica_groups=mesh['igrp'=8,'jgrp'=16] {'jgrp'}, dimensions={2} | all-to-all | bytes 8388608 | tf_op jit(solution)/shard_map/all_to_all | solution.py:22
  704.8 52.8 %all_to_all.104 = bf16[8,64,16,256]{3,2,0,1:T(8,128)(2,1)S(1)} all-to-all(bf16[8,64,16,256]{3,2,0,1:T(8,128)(2,1)S(1)} %copy.96), channel_id=1, replica_groups=mesh['igrp'=8,'jgrp'=16] {'igrp'}, dimensions={1} | all-to-all | bytes 8388608 | tf_op jit(solution)/shard_map/all_to_all | solution.py:23
  758.2 54.4 %all_to_all.105 = bf16[64,8,16,256]{3,2,1,0:T(8,128)(2,1)S(1)} all-to-all(bf16[64,8,16,256]{3,2,1,0:T(8,128)(2,1)S(1)} %bitcast.104), channel_id=1, replica_groups=mesh['igrp'=8,'jgrp'=16] {'jgrp'}, dimensions={0} | all-to-all | bytes 8388608 | tf_op jit(solution)/shard_map/all_to_all | solution.py:24
  828.0 9.1 %copy.100 = f32[8,4,256,256]{3,2,1,0:T(8,128)} copy(f32[8,4,256,256]{2,3,0,1:T(8,128)} %subtract_divide_fusion) | data formatting | bytes 16777216 | tf_op jit(solution)/shard_map/div | solution.py:75
  (122 shorter events, 205.0 us)
Async XLA Ops:
  16.4 5.1 copy-start.4
  16.4 99.7 %all-to-all-start = ((bf16[16,4,256,256]{3,2,1,0:T(8,128)(2,1)}), bf16[16,4,256,256]{3,2,1,0:T(8,128)(2,1)}, u32[]{:S(2)}, u32[]{:S(2)}) async-start(bf16[16,4,256,256]{3,2,1,0:T(8,128)(2,1)} %broadcast_select_fusion.1), calls=%async_computation | async-start | bytes 16777216 | tf_op jit(solution)/shard_map/all_to_all | solution.py:63
  331.5 4.9 copy-start.6
  331.5 69.2 %all-to-all-start.3 = ((bf16[64,8,16,256]{3,2,1,0:T(8,128)(2,1)}), bf16[64,8,16,256]{3,2,1,0:T(8,128)(2,1)}, u32[]{:S(2)}, u32[]{:S(2)}) async-start(bf16[64,8,16,256]{3,2,1,0:T(8,128)(2,1)} %bitcast.97), calls=%async_computation.3 | async-start | bytes 8388608 | tf_op jit(solution)/shard_map/all_to_all | solution.py:24
  336.5 6.2 copy-start.5
  407.5 4.6 copy-start
  407.5 5.9 copy-start.1
  817.2 4.6 copy-start.2
  817.2 5.9 copy-start.3
where the time goes:
time: 839 us; the launch traced here: 837 us
  blocking collectives  377 us (45%)
  local copies, waits for them, and re-layouts  185 us (22%)
  waiting for transfers between devices  151 us (18%)
  matrix products  76.3 us (9%)
  other arithmetic  38 us (5%)
  starting transfers between devices  9.94 us (1%)
    all_to_all x2, blocking collectives, transposed(): lax.all_to_all(cycle_term, 'jgrp', split_axis=2, concat_axis=1, tiled=True)  117 us
    all_to_all x2, blocking collectives, transposed(): lax.all_to_all(section_one, 'igrp', split_axis=1, concat_axis=0, tiled=True)  105 us
    all_to_all x1, blocking collectives, body(): lax.all_to_all(outgoing, 'igrp', split_axis=0, concat_axis=0, tiled=True)  100 us
    gather x16, local copies, waits for them, and re-layouts, per_row(): picked = jnp.take(received, slot_rows, axis=0)  99 us
    all_to_all x1, waiting for transfers between devices, body(): lax.all_to_all(outgoing, 'igrp', split_axis=0, concat_axis=0, tiled=True)  93.2 us
    dot_general x16, matrix products, per_row(): jnp.einsum('mac,mjcb->jab', weight_rows, picked, preferred_element_type=j...  76.3 us
    all_to_all x1, waiting for transfers between devices, transposed(): lax.all_to_all(section_two, 'jgrp', split_axis=0, concat_axis=2, tiled=True)  57.6 us
    all_to_all x1, blocking collectives, transposed(): lax.all_to_all(section_two, 'jgrp', split_axis=0, concat_axis=2, tiled=True)  54.4 us
  transfers between devices with their start and end apart: 2, of which 2 were waited for; matrix products, arithmetic and copies ran while one was open for 1% of the time, Pallas kernels for 0%

commit v1 on v0

v1 whole, which is shorter than its diff:
```python
import functools

import jax
import jax.numpy as jnp
from jax import lax
from jax.experimental import pallas as pl
from jax.experimental.pallas import tpu as pltpu
from jax.sharding import PartitionSpec as P

NNB = 8
CAP = 2
ITERS = 2
MESH = pl.DeviceIdType.MESH
NX, NC, NY, NZ = 4, 2, 4, 4
CHUNKS = 4
ROWS = 8
ORDER = ((2, 0), (1, 0), (3, 0), (2, 1), (1, 1), (3, 1), (0, 1))


def first_true(flags, capacity):
    counted = flags.shape[1]
    ranking = jnp.cumsum(flags.astype(jnp.int32), axis=1) - 1
    offsets = jnp.arange(counted, dtype=jnp.int32)
    hits = flags[:, :, None] & (
        ranking[:, :, None] == jnp.arange(capacity, dtype=jnp.int32)[None, None, :]
    )
    return jnp.sum(offsets[None, :, None] * hits.astype(jnp.int32), axis=1)


def sweep_kernel(
    choice, slot, occ_rows, occ_cols, vir, t_h, k_h, w_h, out_h,
    t_0, t_1, t_2, t_3, k_v, w_v, pk, r_0, r_1, r_2, r_3, cs, b1, b2, fl, eye, stage,
    load_sem, es, er, s1s, s1r, s2s, s2r, s3s, s3r, out_sem,
):
    ig = lax.axis_index("igrp")
    jg = lax.axis_index("jgrp")
    x, c = ig // NC, ig % NC
    y, z = jg // NZ, jg % NZ
    received = (r_0, r_1, r_2, r_3)
    t_v = (t_0, t_1, t_2, t_3)

    def peer(dx, dc):
        return lax.rem(x + dx, NX) * NC + lax.rem(c + dc, NC)

    t_load = [
        pltpu.make_async_copy(t_h.at[:, q], t_v[q], load_sem.at[q]) for q in range(CHUNKS)
    ]
    w_load = pltpu.make_async_copy(w_h, w_v, load_sem.at[CHUNKS])
    k_load = pltpu.make_async_copy(k_h, k_v, load_sem.at[CHUNKS + 1])
    for load in t_load:
        load.start()
    w_load.start()
    k_load.start()

    barrier = pltpu.get_barrier_semaphore()
    inside = z // 2 == c
    for dx, dc in ORDER:
        pl.semaphore_signal(barrier, inc=1, device_id=(peer(dx, dc), jg), device_id_type=MESH)
    for dy in range(1, NY):
        pl.semaphore_signal(
            barrier, inc=1, device_id=(ig, lax.rem(y + dy, NY) * NZ + z), device_id_type=MESH
        )
    for dy in range(NY):
        for h in range(2):
            def greet(dy=dy, h=h):
                pl.semaphore_signal(
                    barrier,
                    inc=1,
                    device_id=(x * NC + z // 2, lax.rem(y + dy, NY) * NZ + 2 * c + h),
                    device_id_type=MESH,
                )
            if dy == 0:
                pl.when(jnp.logical_not(inside & (z == 2 * c + h)))(greet)
            else:
                greet()

    def pack(q):
        t_load[q].wait()

        def one(n, carry):
            kk = n // CAP
            s = n % CAP
            dest = peer(kk // NC, kk % NC)
            pk[q, n] = t_v[q][choice[dest * CAP + s]]
            return carry

        lax.fori_loop(CAP, NX * NC * CAP, one, 0)
        for s in range(CAP):
            received[q][ig * CAP + s] = t_v[q][choice[ig * CAP + s]]

    def exchange(q):
        copies = []
        for dx, dc in ORDER:
            kk = dx * NC + dc
            copies.append(
                pltpu.make_async_remote_copy(
                    src_ref=pk.at[q, pl.ds(kk * CAP, CAP)],
                    dst_ref=received[q].at[pl.ds(ig * CAP, CAP)],
                    send_sem=es.at[q, kk],
                    recv_sem=er.at[q, kk],
                    device_id=(peer(dx, dc), jg),
                    device_id_type=MESH,
                )
            )
        return copies

    def first_stage(q, dy):
        to = lax.rem(y + dy, NY)
        return pltpu.make_async_remote_copy(
            src_ref=cs.at[q, to],
            dst_ref=b1.at[q, y],
            send_sem=s1s.at[q, dy],
            recv_sem=s1r.at[q, dy],
            device_id=(ig, to * NZ + z),
            device_id_type=MESH,
        )

    def second_stage(q, dx):
        to = lax.rem(x + dx, NX)
        return pltpu.make_async_remote_copy(
            src_ref=b1.at[q, to],
            dst_ref=b2.at[q, x],
            send_sem=s2s.at[q, dx],
            recv_sem=s2r.at[q, dx],
            device_id=(to * NC + c, jg),
            device_id_type=MESH,
        )

    def third_stage(q, dx, h):
        source = lax.rem(x + NX - dx, NX)
        own = inside & (source == y) & (z == 2 * c + h)

        def remote():
            return pltpu.make_async_remote_copy(
                src_ref=b2.at[q, source, h],
                dst_ref=fl.at[q, z % 2, y],
                send_sem=s3s.at[q, dx, h],
                recv_sem=s3r.at[q, z % 2, y],
                device_id=(x * NC + z // 2, source * NZ + 2 * c + h),
                device_id_type=MESH,
            )

        def local():
            return pltpu.make_async_copy(
                b2.at[q, source, h], fl.at[q, z % 2, y], s3r.at[q, z % 2, y]
            )

        return own, remote, local

    def forward(q):
        for dy in range(1, NY):
            first_stage(q, dy).wait_recv()
        b2[q, x] = b1[q, x]
        for dx in range(1, NX):
            second_stage(q, dx).start()

    def finish(q):
        for half in range(2):
            for col in range(4):
                block = fl.at[q, half, col]
                pltpu.make_async_copy(block, block, s3r.at[q, half, col]).wait()
        update(q)

    def compute(q):
        blocks = received[q]

        def per_row(i, carry):
            total = jnp.zeros((256, 256), jnp.float32)
            for m in range(NNB):
                total += jnp.dot(
                    w_v[i, m], blocks[slot[i * NNB + m]], preferred_element_type=jnp.float32
                )
            cs[q, i % 4, i // 4] = total.astype(jnp.bfloat16)
            return carry

        lax.fori_loop(0, ROWS, per_row, 0)

    def update(q):
        def per_pair(n, carry):
            half = n // 4
            col = n % 4
            row = 4 * half + q
            flipped = lax.dot_general(
                eye[...], fl[q, half, col], (((1,), (1,)), ((), ())),
                preferred_element_type=jnp.float32,
            )
            total = (
                k_v[row, col].astype(jnp.float32) + cs[col, q, half].astype(jnp.float32) + flipped
            )
            value = total / (vir[...] - occ_rows[row] - occ_cols[col])
            stage[q, half, col] = value.astype(stage.dtype)
            return carry

        lax.fori_loop(0, 8, per_pair, 0)
        for half in range(2):
            out_copy(q, half).start()

    def out_copy(q, half):
        return pltpu.make_async_copy(
            stage.at[q, half], out_h.at[4 * half + q], out_sem.at[q, half]
        )

    rows_of = lax.broadcasted_iota(jnp.int32, (256, 256), 0)
    cols_of = lax.broadcasted_iota(jnp.int32, (256, 256), 1)
    eye[...] = jnp.where(rows_of == cols_of, 1.0, 0.0).astype(jnp.bfloat16)
    pack(0)
    pl.semaphore_wait(barrier, 18 - inside.astype(jnp.int32))

    for q in range(CHUNKS):
        if q + 1 < CHUNKS:
            pack(q + 1)
        for copy in exchange(q):
            copy.start()

    w_load.wait()
    for q in range(CHUNKS):
        for copy in exchange(q):
            copy.wait_recv()
        compute(q)
        b1[q, y] = cs[q, y]
        for dy in range(1, NY):
            first_stage(q, dy).start()
        if q >= 1:
            forward(q - 1)
    forward(CHUNKS - 1)
    k_load.wait()
    for q in range(CHUNKS):
        for dx in range(NX):
            if dx > 0:
                second_stage(q, dx).wait_recv()
            for h in range(2):
                own, remote, local = third_stage(q, dx, h)
                pl.when(jnp.logical_not(own))(lambda remote=remote: remote().start())
                pl.when(own)(lambda local=local: local().start())
        if q >= 1:
            finish(q - 1)
    finish(CHUNKS - 1)

    for q in range(CHUNKS):
        for copy in exchange(q):
            copy.wait_send()
        for dy in range(1, NY):
            first_stage(q, dy).wait_send()
        for dx in range(1, NX):
            second_stage(q, dx).wait_send()
        for dx in range(NX):
            for h in range(2):
                own, remote, local = third_stage(q, dx, h)
                pl.when(jnp.logical_not(own))(lambda remote=remote: remote().wait_send())
        for half in range(2):
            out_copy(q, half).wait()


def sweep(call_id, dtype, choice, slot, occ_rows, occ_cols, vir, current, integrals, weights):
    block = (256, 256)
    bf16 = jnp.bfloat16
    smem = pl.BlockSpec(memory_space=pltpu.SMEM)
    anywhere = pl.BlockSpec(memory_space=pl.ANY)
    dma = pltpu.SemaphoreType.DMA
    return pl.pallas_call(
        sweep_kernel,
        out_shape=jax.ShapeDtypeStruct((ROWS, CHUNKS) + block, dtype),
        in_specs=[smem] * 4 + [pl.BlockSpec(memory_space=pltpu.VMEM)] + [anywhere] * 3,
        out_specs=anywhere,
        scratch_shapes=[pltpu.VMEM((ROWS,) + block, bf16)] * CHUNKS
        + [
            pltpu.VMEM((ROWS, CHUNKS) + block, bf16),
            pltpu.VMEM((ROWS, NNB) + block, bf16),
            pltpu.VMEM((CHUNKS, NX * NC * CAP) + block, bf16),
        ]
        + [pltpu.VMEM((NX * NC * CAP,) + block, bf16)] * CHUNKS
        + [pltpu.VMEM((CHUNKS, 4, 2) + block, bf16)] * 3
        + [
            pltpu.VMEM((CHUNKS, 2, 4) + block, bf16),
            pltpu.VMEM(block, bf16),
            pltpu.VMEM((CHUNKS, 2, 4) + block, dtype),
            dma((CHUNKS + 2,)),
            dma((CHUNKS, 8)),
            dma((CHUNKS, 8)),
            dma((CHUNKS, 4)),
            dma((CHUNKS, 4)),
            dma((CHUNKS, 4)),
            dma((CHUNKS, 4)),
            dma((CHUNKS, 4, 2)),
            dma((CHUNKS, 2, 4)),
            dma((CHUNKS, 2)),
        ],
        compiler_params=pltpu.CompilerParams(
            collective_id=call_id, has_side_effects=True, vmem_limit_bytes=67043328
        ),
        name=f"sweep_{call_id}",
    )(choice, slot, occ_rows, occ_cols, vir, current, integrals, weights)


def body(t_start, integrals, weights, neighbours, eps_occ, eps_vir):
    row_count = weights.shape[0]
    col_count = t_start.shape[1]
    capacity = CAP
    igroups = lax.axis_size("igrp")
    my_igrp = lax.axis_index("igrp")
    my_jgrp = lax.axis_index("jgrp")
    grouped = neighbours.reshape(igroups, row_count * NNB)
    own_orbitals = my_igrp * row_count + jnp.arange(row_count, dtype=jnp.int32)
    wanted = jnp.any(grouped[:, :, None] == own_orbitals[None, None, :], axis=1)
    send_choice = first_true(wanted, capacity).reshape(-1)
    my_rows = lax.dynamic_slice_in_dim(neighbours, my_igrp * row_count, row_count, 0)
    flat_list = my_rows.reshape(-1)
    all_blocks = jnp.arange(igroups * row_count, dtype=jnp.int32).reshape(igroups, row_count)
    needed = jnp.any(flat_list[None, None, :] == all_blocks[:, :, None], axis=2)
    recv_orbitals = (
        first_true(needed, capacity) + (jnp.arange(igroups, dtype=jnp.int32) * row_count)[:, None]
    ).reshape(-1)
    slot_index = jnp.sum(
        jnp.arange(igroups * capacity, dtype=jnp.int32)[None, None, :]
        * (my_rows[:, :, None] == recv_orbitals[None, None, :]).astype(jnp.int32),
        axis=2,
    ).reshape(-1)
    occ_rows = lax.dynamic_slice_in_dim(eps_occ, my_igrp * row_count, row_count, 0)
    occ_cols = lax.dynamic_slice_in_dim(eps_occ, my_jgrp * col_count, col_count, 0)
    vir = eps_vir[:, None] + eps_vir[None, :]
    current = t_start
    for step in range(ITERS):
        dtype = jnp.float32 if step == ITERS - 1 else jnp.bfloat16
        current = sweep(
            step, dtype, send_choice, slot_index, occ_rows, occ_cols, vir, current, integrals, weights
        )
    return current


def solution(mesh):
    placed = (
        P("igrp", "jgrp", None, None),
        P("igrp", "jgrp", None, None),
        P("igrp", None, None, None),
        P(),
        P(),
        P(),
    )
    return jax.shard_map(
        body, mesh=mesh, in_specs=placed, out_specs=P("igrp", "jgrp", None, None), check_vma=False
    )
```

time: 839 us -> 368 us (0.44)
  blocking collectives: 377 us -> 0 us
  Pallas kernels: 0 us -> 350 us
  local copies, waits for them, and re-layouts: 185 us -> 13.6 us
  waiting for transfers between devices: 151 us -> 0 us
  matrix products: 76.3 us -> 0 us
  other arithmetic: 38 us -> 3.09 us
  starting transfers between devices: 9.94 us -> 0 us
    all_to_all x6 -> x0, blocking collectives: 377 us -> none  [the longest x2 117 us: transposed(): lax.all_to_all(cycle_term, 'jgrp', split_axis=2, concat_axis=1, tiled=True)]
    pallas_call x0 -> x2, Pallas kernels: none -> 350 us  [sweep(): pl.pallas_call(sweep_kernel, out_shape=jax.ShapeDtypeStruct((ROWS, CHUNKS...]
    all_to_all x2 -> x0, waiting for transfers between devices: 151 us -> none  [the longest x1 93.2 us: body(): lax.all_to_all(outgoing, 'igrp', split_axis=0, concat_axis=0, tiled=True)]
    gather x18 -> x0, local copies, waits for them, and re-layouts: 113 us -> none  [the longest x16 99 us: per_row(): picked = jnp.take(received, slot_rows, axis=0)]
    dot_general x16 -> x0, matrix products: 76.3 us -> none  [per_row(): jnp.einsum('mac,mjcb->jab', weight_rows, picked, preferred_element_type=j...]
    while x3 -> x0, local copies, waits for them, and re-layouts: 27.9 us -> none  [body(): lax.scan(per_row, jnp.zeros((), jnp.int32), (weights, slot_index))]
    convert_element_type x3 -> x0, other arithmetic: 15.7 us -> none  [the longest x2 11.4 us: body(): flipped.astype(jnp.float32)]
    select_n x3 -> x0, other arithmetic: 15.3 us -> none  [body(): outgoing = jnp.take(current, send_choice, axis=0)]
  transfers between devices with their start and end apart: 2 -> 0, of which waited for: 2 -> 0; matrix products, arithmetic and copies ran while one was open for 1% -> 0% of each run, Pallas kernels for 0% -> 0%
where the time goes in v1:
time: 368 us; the launch traced here: 366 us
  Pallas kernels  350 us (95%)
  local copies, waits for them, and re-layouts  13.6 us (4%)
    pallas_call x2, Pallas kernels, sweep(): pl.pallas_call(sweep_kernel, out_shape=jax.ShapeDtypeStruct((ROWS, CHUNKS...  350 us
    unnamed x2, local copies, waits for them, and re-layouts  8.42 us

profile of v1, /device:TPU:0, one launch (start us, length us, event | category | flops | bytes accessed | tf_op | source)
XLA Modules:
  0.0 366.2 jit_solution(16642241642643212412)
XLA Ops:
  0.0 1.3 dynamic_slice.11.occ_cols
  1.3 1.3 dynamic_slice.10.occ_rows
  2.6 0.8 constant_dynamic-slice_fusion
  3.4 0.1 copy.14
  3.5 0.1 eq.77
  3.5 0.3 compare_reduce_fusion
  3.8 0.2 reduce_window_sum.18
  4.0 0.2 select_reduce_fusion.1
  4.2 0.1 copy.16
  4.3 0.1 add.66
  4.3 0.3 select_reduce_fusion
  4.6 0.7 reshape.62.slot
  5.3 0.8 copy.12
  6.1 0.1 eq.34
  6.1 0.3 compare_reduce_fusion.1
  6.4 0.2 reduce_window_sum.17
  6.6 0.2 select_reduce_fusion.2
  6.8 0.1 copy.13
  6.8 0.6 reshape.61.choice
  7.5 1.6 broadcast_add_fusion.vir
  9.0 172.0 %sweep_0.1.t_h = bf16[8,4,256,256]{3,2,1,0:T(8,128)(2,1)} custom-call(s32[16]{0:T(128)} %reshape.61.choice, s32[64]{0:T(128)} %reshape.62.slot, f32[8]{0:T(128)} %dynamic_slice.10.occ_rows, f32[4]{0:T(128)} %dynamic_slice.11.occ_cols, f32[256,256]{1,0:T(8,128)} %broadcast_add_fusion.vir, bf16[8,4,256,256]{3,2,1,0:T(8,128)(2,1)} %t_h.1, ...), custom_call_target="tpu_custom_call" | custom-call | tf_op jit(solution)/shard_map/sweep_0/pallas_call | solution.py:260
  181.0 177.5 %sweep_1.1 = f32[8,4,256,256]{3,2,1,0:T(8,128)} custom-call(s32[16]{0:T(128)} %reshape.61.choice, s32[64]{0:T(128)} %reshape.62.slot, f32[8]{0:T(128)} %dynamic_slice.10.occ_rows, f32[4]{0:T(128)} %dynamic_slice.11.occ_cols, f32[256,256]{1,0:T(8,128)} %broadcast_add_fusion.vir, bf16[8,4,256,256]{3,2,1,0:T(8,128)(2,1)} %sweep_0.1.t_h, ...), custom_call_target="tpu_custom_call" | custom-call | tf_op jit(solution)/shard_map/sweep_1/pallas_call | solution.py:260
  358.6 7.7 %copy.18 = f32[8,4,256,256]{3,2,1,0:T(8,128)} copy(f32[8,4,256,256]{3,2,1,0:T(8,128)} %sweep_1.1) | data formatting | bytes 16777216
  (8 shorter events, 0.0 us)

commit v2 on v1

v2 whole, which is shorter than its diff:
```python
import functools

import jax
import jax.numpy as jnp
from jax import lax
from jax.experimental import pallas as pl
from jax.experimental.pallas import tpu as pltpu
from jax.sharding import PartitionSpec as P

NNB = 8
CAP = 2
ITERS = 2
MESH = pl.DeviceIdType.MESH
NX, NC, NY, NZ = 4, 2, 4, 4
CHUNKS = 4
ROWS = 8
ORDER = ((2, 0), (1, 0), (3, 0), (2, 1), (1, 1), (3, 1), (0, 1))


def sweeps_kernel(
    masks, listed, occ, eps, t_h, k_h, w_h, out_h,
    t_0, t_1, t_2, t_3, k_v, w_v, pk, r_0, r_1, r_2, r_3, cs, b1, b2, fl, eye, vir, stage,
    choice, slot, load_sem, es, er, s1s, s1r, s2s, s2r, s3s, s3r, out_sem, free,
):
    ig = lax.axis_index("igrp")
    jg = lax.axis_index("jgrp")
    x, c = ig // NC, ig % NC
    y, z = jg // NZ, jg % NZ
    received = (r_0, r_1, r_2, r_3)
    t_v = (t_0, t_1, t_2, t_3)

    def peer(dx, dc):
        return lax.rem(x + dx, NX) * NC + lax.rem(c + dc, NC)

    t_load = [
        pltpu.make_async_copy(t_h.at[:, q], t_v[q], load_sem.at[q]) for q in range(CHUNKS)
    ]
    w_load = pltpu.make_async_copy(w_h, w_v, load_sem.at[CHUNKS])
    k_load = pltpu.make_async_copy(k_h, k_v, load_sem.at[CHUNKS + 1])
    for load in t_load:
        load.start()

    barrier = pltpu.get_barrier_semaphore()
    inside = z // 2 == c
    for dx, dc in ORDER:
        pl.semaphore_signal(barrier, inc=1, device_id=(peer(dx, dc), jg), device_id_type=MESH)
    for dy in range(1, NY):
        pl.semaphore_signal(
            barrier, inc=1, device_id=(ig, lax.rem(y + dy, NY) * NZ + z), device_id_type=MESH
        )
    def meet(dy, h, sem):
        def greet():
            pl.semaphore_signal(
                sem,
                inc=1,
                device_id=(x * NC + z // 2, lax.rem(y + dy, NY) * NZ + 2 * c + h),
                device_id_type=MESH,
            )

        if dy == 0:
            pl.when(jnp.logical_not(inside & (z == 2 * c + h)))(greet)
        else:
            greet()

    for dy in range(NY):
        for h in range(2):
            meet(dy, h, barrier)

    def place(bit):
        found = jnp.int32(0)
        for k in range(1, ROWS):
            found += (bit >= (1 << k)).astype(jnp.int32)
        return found

    def choose(p, carry):
        mask = masks[p, ig]
        low = mask & (0 - mask)
        choice[p * CAP] = place(low)
        choice[p * CAP + 1] = place(mask - low)
        return carry

    def locate(n, carry):
        orbital = listed[n % NNB, ig * ROWS + n // NNB]
        block = orbital // ROWS
        below = masks[ig, block] % lax.shift_left(jnp.int32(1), orbital % ROWS)
        slot[n] = block * CAP + (below > 0).astype(jnp.int32)
        return carry

    def pack(q):
        def one(n, carry):
            kk = n // CAP
            s = n % CAP
            dest = peer(kk // NC, kk % NC)
            pk[q, n] = t_v[q][choice[dest * CAP + s]]
            return carry

        lax.fori_loop(CAP, NX * NC * CAP, one, 0)
        for s in range(CAP):
            received[q][ig * CAP + s] = t_v[q][choice[ig * CAP + s]]

    def exchange(q):
        copies = []
        for dx, dc in ORDER:
            kk = dx * NC + dc
            copies.append(
                pltpu.make_async_remote_copy(
                    src_ref=pk.at[q, pl.ds(kk * CAP, CAP)],
                    dst_ref=received[q].at[pl.ds(ig * CAP, CAP)],
                    send_sem=es.at[q, kk],
                    recv_sem=er.at[q, kk],
                    device_id=(peer(dx, dc), jg),
                    device_id_type=MESH,
                )
            )
        return copies

    def start(copies):
        own, remote, local = copies
        pl.when(jnp.logical_not(own))(lambda: remote().start())
        pl.when(own)(lambda: local().start())

    def sent(copies):
        own, remote, local = copies
        pl.when(jnp.logical_not(own))(lambda: remote().wait_send())

    def landed(block, sem):
        pltpu.make_async_copy(block, block, sem).wait()

    def first_stage(q, dy, h):
        to = lax.rem(y + dy, NY)
        own = inside & (z == 2 * c + h) if dy == 0 else None
        source, target, arrival = cs.at[q, to, h], b1.at[q, y, z % 2], s1r.at[q, y, z % 2]

        def remote():
            return pltpu.make_async_remote_copy(
                src_ref=source,
                dst_ref=target,
                send_sem=s1s.at[q, dy, h],
                recv_sem=arrival,
                device_id=(x * NC + z // 2, to * NZ + 2 * c + h),
                device_id_type=MESH,
            )

        return own, remote, lambda: pltpu.make_async_copy(source, target, arrival)

    def second_stage(q, dx):
        to = lax.rem(x + dx, NX)
        return pltpu.make_async_remote_copy(
            src_ref=b1.at[q, to],
            dst_ref=b2.at[q, x],
            send_sem=s2s.at[q, dx],
            recv_sem=s2r.at[q, dx],
            device_id=(to * NC + c, jg),
            device_id_type=MESH,
        )

    def third_stage(q, dx):
        to = lax.rem(x + NX - dx, NX)
        source, target, arrival = b2.at[q, to], fl.at[q, y], s3r.at[q, y]

        def remote():
            return pltpu.make_async_remote_copy(
                src_ref=source,
                dst_ref=target,
                send_sem=s3s.at[q, dx],
                recv_sem=arrival,
                device_id=(ig, to * NZ + z),
                device_id_type=MESH,
            )

        return to == y, remote, lambda: pltpu.make_async_copy(source, target, arrival)

    def settle(q):
        for dy in range(NY):
            for h in range(2):
                copies = first_stage(q, dy, h)
                if dy == 0:
                    sent(copies)
                else:
                    copies[1]().wait_send()
        for dx in range(1, NX):
            second_stage(q, dx).wait_send()
        for dx in range(NX):
            sent(third_stage(q, dx))

    def spread(q):
        for dy in (2, 1, 3, 0):
            for h in range(2):
                copies = first_stage(q, dy, h)
                if dy == 0:
                    start(copies)
                else:
                    copies[1]().start()

    def forward(q):
        for col in range(NY):
            for half in range(2):
                landed(b1.at[q, col, half], s1r.at[q, col, half])
        b2[q, x] = b1[q, x]
        for dx in (2, 1, 3):
            second_stage(q, dx).start()

    def deliver(q):
        for dx in (0, 2, 1, 3):
            if dx > 0:
                second_stage(q, dx).wait_recv()
            start(third_stage(q, dx))

    def finish(q, last):
        for col in range(NY):
            landed(fl.at[q, col], s3r.at[q, col])
        update(q, last)

    def compute(q):
        blocks = received[q]

        def per_row(i, carry):
            total = jnp.zeros((256, 256), jnp.float32)
            for m in range(NNB):
                total += jnp.dot(
                    w_v[i, m], blocks[slot[i * NNB + m]], preferred_element_type=jnp.float32
                )
            cs[q, i % 4, i // 4] = total.astype(jnp.bfloat16)
            return carry

        lax.fori_loop(0, ROWS, per_row, 0)

    def update(q, last):
        def per_pair(col, half, carry):
            row = 4 * half + q
            flipped = lax.dot_general(
                eye[...], fl[q, col, half], (((1,), (1,)), ((), ())),
                preferred_element_type=jnp.float32,
            )
            total = (
                k_v[row, col].astype(jnp.float32) + cs[col, q, half].astype(jnp.float32) + flipped
            )
            value = total / (vir[...] - occ[ig * ROWS + row] - occ[jg * CHUNKS + col])
            if last:
                stage[q, half, col] = value
            else:
                t_v[col][row] = value.astype(jnp.bfloat16)
            return carry

        for col in range(CHUNKS):
            lax.fori_loop(0, 2, functools.partial(per_pair, col), 0)
        if last:
            for half in range(2):
                out_copy(q, half).start()

    def out_copy(q, half):
        return pltpu.make_async_copy(
            stage.at[q, half], out_h.at[4 * half + q], out_sem.at[q, half]
        )

    def release(index, devices):
        for device in devices:
            pl.semaphore_signal(free.at[index], inc=1, device_id=device, device_id_type=MESH)

    x_peers = [(lax.rem(x + dx, NX) * NC + c, jg) for dx in range(1, NX)]
    y_peers = [(ig, lax.rem(y + dy, NY) * NZ + z) for dy in range(1, NY)]
    ring_peers = [(peer(dx, dc), jg) for dx, dc in ORDER]

    rows_of = lax.broadcasted_iota(jnp.int32, (256, 256), 0)
    cols_of = lax.broadcasted_iota(jnp.int32, (256, 256), 1)
    eye[...] = jnp.where(rows_of == cols_of, 1.0, 0.0).astype(jnp.bfloat16)
    across = jnp.broadcast_to(eps[...], (256, 256))
    vir[...] = across + across.T
    lax.fori_loop(0, NX * NC, choose, 0)
    lax.fori_loop(0, ROWS * NNB, locate, 0)
    for q in range(CHUNKS):
        t_load[q].wait()
        pack(q)
    pl.semaphore_wait(barrier, 18 - inside.astype(jnp.int32))

    for step in range(ITERS):
        first, last = step == 0, step == ITERS - 1
        if not first:
            for q in range(CHUNKS):
                for copy in exchange(q):
                    copy.wait_send()
            pl.semaphore_wait(free.at[0], len(ORDER))
            pack(0)
        for q in range(CHUNKS - 1):
            if not first:
                pack(q + 1)
            for copy in exchange(q):
                copy.start()
        if first:
            w_load.start()
            k_load.start()
            w_load.wait()
        else:
            for q in range(CHUNKS):
                settle(q)
            release(2, x_peers)
            release(3, y_peers)
            for dy in range(NY):
                for h in range(2):
                    meet(dy, h, free.at[1])
        for q in range(CHUNKS):
            for copy in exchange(q):
                copy.wait_recv()
            compute(q)
            if not first and q == 0:
                pl.semaphore_wait(free.at[1], 8 - inside.astype(jnp.int32))
            spread(q)
            if q >= 1:
                if not first and q == 1:
                    pl.semaphore_wait(free.at[2], NX - 1)
                forward(q - 1)
            if q == 1:
                for copy in exchange(CHUNKS - 1):
                    copy.start()
            if q == 2:
                if first:
                    k_load.wait()
                else:
                    pl.semaphore_wait(free.at[3], NY - 1)
                deliver(0)
        if not last:
            release(0, ring_peers)
        deliver(1)
        finish(0, last)
        forward(3)
        deliver(2)
        finish(1, last)
        deliver(3)
        finish(2, last)
        finish(3, last)

    for q in range(CHUNKS):
        for copy in exchange(q):
            copy.wait_send()
        settle(q)
        for half in range(2):
            out_copy(q, half).wait()


def body(t_start, integrals, weights, neighbours, eps_occ, eps_vir):
    block = (256, 256)
    bf16 = jnp.bfloat16
    smem = pl.BlockSpec(memory_space=pltpu.SMEM)
    anywhere = pl.BlockSpec(memory_space=pl.ANY)
    dma = pltpu.SemaphoreType.DMA
    listed = neighbours.T
    bits = jnp.where(
        (listed // ROWS)[:, :, None] == jnp.arange(NX * NC, dtype=jnp.int32),
        lax.shift_left(jnp.int32(1), listed % ROWS)[:, :, None],
        0,
    ).reshape(NNB, NX * NC, ROWS, NX * NC)
    masks = lax.reduce(bits, jnp.int32(0), lax.bitwise_or, (0, 2))
    return pl.pallas_call(
        sweeps_kernel,
        out_shape=jax.ShapeDtypeStruct((ROWS, CHUNKS) + block, jnp.float32),
        in_specs=[smem] * 3 + [pl.BlockSpec(memory_space=pltpu.VMEM)] + [anywhere] * 3,
        out_specs=anywhere,
        scratch_shapes=[pltpu.VMEM((ROWS,) + block, bf16)] * CHUNKS
        + [
            pltpu.VMEM((ROWS, CHUNKS) + block, bf16),
            pltpu.VMEM((ROWS, NNB) + block, bf16),
            pltpu.VMEM((CHUNKS, NX * NC * CAP) + block, bf16),
        ]
        + [pltpu.VMEM((NX * NC * CAP,) + block, bf16)] * CHUNKS
        + [pltpu.VMEM((CHUNKS, 4, 2) + block, bf16)] * 4
        + [
            pltpu.VMEM(block, bf16),
            pltpu.VMEM(block, jnp.float32),
            pltpu.VMEM((CHUNKS, 2, 4) + block, jnp.float32),
            pltpu.SMEM((NX * NC * CAP,), jnp.int32),
            pltpu.SMEM((ROWS * NNB,), jnp.int32),
            dma((CHUNKS + 2,)),
            dma((CHUNKS, 8)),
            dma((CHUNKS, 8)),
            dma((CHUNKS, 4, 2)),
            dma((CHUNKS, 4, 2)),
            dma((CHUNKS, 4)),
            dma((CHUNKS, 4)),
            dma((CHUNKS, 4)),
            dma((CHUNKS, 4)),
            dma((CHUNKS, 2)),
            pltpu.SemaphoreType.REGULAR((4,)),
        ],
        compiler_params=pltpu.CompilerParams(
            collective_id=0, has_side_effects=True, vmem_limit_bytes=67043328
        ),
        name="sweeps",
    )(masks, listed, eps_occ, eps_vir.reshape(1, 256), t_start, integrals, weights)


def solution(mesh):
    placed = (
        P("igrp", "jgrp", None, None),
        P("igrp", "jgrp", None, None),
        P("igrp", None, None, None),
        P(),
        P(),
        P(),
    )
    return jax.shard_map(
        body, mesh=mesh, in_specs=placed, out_specs=P("igrp", "jgrp", None, None), check_vma=False
    )
```

time: 368 us -> 335 us (0.910)
  Pallas kernels: 350 us -> 321 us
  local copies, waits for them, and re-layouts: 13.6 us -> 7.8 us
    pallas_call x2 -> x1, Pallas kernels: 350 us -> 321 us  [body(): pl.pallas_call(sweeps_kernel, out_shape=jax.ShapeDtypeStruct((ROWS, CHUNK...]
    unnamed x2 -> x1, local copies, waits for them, and re-layouts: 8.42 us -> 7.65 us
where the time goes in v2:
time: 335 us; the launch traced here: 330 us
  Pallas kernels  321 us (96%)
  local copies, waits for them, and re-layouts  7.8 us (2%)
    pallas_call x1, Pallas kernels, body(): pl.pallas_call(sweeps_kernel, out_shape=jax.ShapeDtypeStruct((ROWS, CHUNK...  321 us
    unnamed x1, local copies, waits for them, and re-layouts  7.65 us

profile of v2, /device:TPU:0, one launch (start us, length us, event | category | flops | bytes accessed | tf_op | source)
XLA Modules:
  0.0 329.9 jit_solution(10665615695574046552)
XLA Ops:
  0.0 0.7 add_select_fusion.1
  0.7 0.1 eq.18
  0.8 0.1 broadcast_in_dim.17
  0.8 0.8 select_reduce_fusion.masks
  1.7 320.6 %sweeps.1 = f32[8,4,256,256]{3,2,1,0:T(8,128)} custom-call(s32[8,8]{1,0:T(8,128)} %select_reduce_fusion.masks, s32[8,64]{1,0:T(8,128)} %bitcast.4, f32[64]{0:T(128)} %occ.1, f32[1,256]{1,0:T(1,128)} %bitcast.5, bf16[8,4,256,256]{3,2,1,0:T(8,128)(2,1)} %t_h.1, bf16[8,4,256,256]{3,2,1,0:T(8,128)(2,1)} %k_h.1, bf16[8,8,256,256]{3,2,1,0:T(8,128)(2,1)} %w_h.1), custom_call_target="tpu_custom_call" | custom-call | tf_op jit(solution)/shard_map/sweeps/pallas_call | solution.py:353
  322.3 7.7 %copy.8 = f32[8,4,256,256]{3,2,1,0:T(8,128)} copy(f32[8,4,256,256]{3,2,1,0:T(8,128)} %sweeps.1) | data formatting | bytes 16777216

commit v3 on v2

--- a/solution.py
+++ b/solution.py
@@ -12,31 +12,47 @@
 ITERS = 2
 MESH = pl.DeviceIdType.MESH
 NX, NC, NY, NZ = 4, 2, 4, 4
-CHUNKS = 4
+COLS = 4
 ROWS = 8
+CHUNKS = ((0, 0, 256), (1, 0, 256), (2, 0, 256), (3, 0, 128), (3, 128, 128))
+COUNT = len(CHUNKS)
+WHOLE = 3
+SCHEDULE = (
+    "E0", "E1", "E2", "C0", "C1", "F0", "E3", "E4", "C2", "F1", "D0", "C3",
+    "F2", "C4", "F3", "D1", "U0", "F4", "D2", "U1", "D3", "U2", "D4", "U3",
+    "U4",
+)
+SPREAD = (2, 1, 3, 0)
 ORDER = ((2, 0), (1, 0), (3, 0), (2, 1), (1, 1), (3, 1), (0, 1))
 
 
 def sweeps_kernel(
-    masks, listed, occ, eps, t_h, k_h, w_h, out_h,
-    t_0, t_1, t_2, t_3, k_v, w_v, pk, r_0, r_1, r_2, r_3, cs, b1, b2, fl, eye, vir, stage,
-    choice, slot, load_sem, es, er, s1s, s1r, s2s, s2r, s3s, s3r, out_sem, free,
+    masks, listed, occ, eps, t_h, k_h, w_h, out_v,
+    t_0, t_1, t_2, t_3, k_v, w_v, r_0, r_1, r_2, r_3, r_4,
+    pk_w, cs_w, b1_w, b2_w, fl_w, pk_p, cs_p, b1_p, b2_p, fl_p, eye, vir,
+    choice, slot, load_sem, es, er, s1s, s1r, s2s, s2r, s3s, s3r, free,
 ):
     ig = lax.axis_index("igrp")
     jg = lax.axis_index("jgrp")
     x, c = ig // NC, ig % NC
     y, z = jg // NZ, jg % NZ
-    received = (r_0, r_1, r_2, r_3)
+    received = (r_0, r_1, r_2, r_3, r_4)
+
+    def of(whole, part):
+        return [whole.at[q] if q < WHOLE else part.at[q - WHOLE] for q in range(COUNT)]
+
+    pk, cs, b1 = of(pk_w, pk_p), of(cs_w, cs_p), of(b1_w, b1_p)
+    b2, fl = of(b2_w, b2_p), of(fl_w, fl_p)
     t_v = (t_0, t_1, t_2, t_3)
 
     def peer(dx, dc):
         return lax.rem(x + dx, NX) * NC + lax.rem(c + dc, NC)
 
     t_load = [
-        pltpu.make_async_copy(t_h.at[:, q], t_v[q], load_sem.at[q]) for q in range(CHUNKS)
+        pltpu.make_async_copy(t_h.at[:, q], t_v[q], load_sem.at[q]) for q in range(COLS)
     ]
-    w_load = pltpu.make_async_copy(w_h, w_v, load_sem.at[CHUNKS])
-    k_load = pltpu.make_async_copy(k_h, k_v, load_sem.at[CHUNKS + 1])
+    w_load = pltpu.make_async_copy(w_h, w_v, load_sem.at[COLS])
+    k_load = pltpu.make_async_copy(k_h, k_v, load_sem.at[COLS + 1])
     for load in t_load:
         load.start()
 
@@ -87,16 +103,18 @@
         return carry
 
     def pack(q):
+        col, lo, width = CHUNKS[q]
+
         def one(n, carry):
             kk = n // CAP
             s = n % CAP
             dest = peer(kk // NC, kk % NC)
-            pk[q, n] = t_v[q][choice[dest * CAP + s]]
+            pk[q][n] = t_v[col][choice[dest * CAP + s], :, lo : lo + width]
             return carry
 
         lax.fori_loop(CAP, NX * NC * CAP, one, 0)
         for s in range(CAP):
-            received[q][ig * CAP + s] = t_v[q][choice[ig * CAP + s]]
+            received[q][ig * CAP + s] = t_v[col][choice[ig * CAP + s], :, lo : lo + width]
 
     def exchange(q):
         copies = []
@@ -104,7 +122,7 @@
             kk = dx * NC + dc
             copies.append(
                 pltpu.make_async_remote_copy(
-                    src_ref=pk.at[q, pl.ds(kk * CAP, CAP)],
+                    src_ref=pk[q].at[pl.ds(kk * CAP, CAP)],
                     dst_ref=received[q].at[pl.ds(ig * CAP, CAP)],
                     send_sem=es.at[q, kk],
                     recv_sem=er.at[q, kk],
@@ -129,7 +147,7 @@
     def first_stage(q, dy, h):
         to = lax.rem(y + dy, NY)
         own = inside & (z == 2 * c + h) if dy == 0 else None
-        source, target, arrival = cs.at[q, to, h], b1.at[q, y, z % 2], s1r.at[q, y, z % 2]
+        source, target, arrival = cs[q].at[to, h], b1[q].at[y, z % 2], s1r.at[q, y, z % 2]
 
         def remote():
             return pltpu.make_async_remote_copy(
@@ -146,8 +164,8 @@
     def second_stage(q, dx):
         to = lax.rem(x + dx, NX)
         return pltpu.make_async_remote_copy(
-            src_ref=b1.at[q, to],
-            dst_ref=b2.at[q, x],
+            src_ref=b1[q].at[to],
+            dst_ref=b2[q].at[x],
             send_sem=s2s.at[q, dx],
             recv_sem=s2r.at[q, dx],
             device_id=(to * NC + c, jg),
@@ -156,7 +174,7 @@
 
     def third_stage(q, dx):
         to = lax.rem(x + NX - dx, NX)
-        source, target, arrival = b2.at[q, to], fl.at[q, y], s3r.at[q, y]
+        source, target, arrival = b2[q].at[to], fl[q].at[y], s3r.at[q, y]
 
         def remote():
             return pltpu.make_async_remote_copy(
@@ -184,7 +202,7 @@
             sent(third_stage(q, dx))
 
     def spread(q):
-        for dy in (2, 1, 3, 0):
+        for dy in SPREAD:
             for h in range(2):
                 copies = first_stage(q, dy, h)
                 if dy == 0:
@@ -195,8 +213,8 @@
     def forward(q):
         for col in range(NY):
             for half in range(2):
-                landed(b1.at[q, col, half], s1r.at[q, col, half])
-        b2[q, x] = b1[q, x]
+                landed(b1[q].at[col, half], s1r.at[q, col, half])
+        b2[q][x] = b1[q][x]
         for dx in (2, 1, 3):
             second_stage(q, dx).start()
 
@@ -208,50 +226,52 @@
 
     def finish(q, last):
         for col in range(NY):
-            landed(fl.at[q, col], s3r.at[q, col])
+            landed(fl[q].at[col], s3r.at[q, col])
         update(q, last)
 
     def compute(q):
         blocks = received[q]
 
         def per_row(i, carry):
-            total = jnp.zeros((256, 256), jnp.float32)
+            total = jnp.zeros((256, CHUNKS[q][2]), jnp.float32)
             for m in range(NNB):
                 total += jnp.dot(
                     w_v[i, m], blocks[slot[i * NNB + m]], preferred_element_type=jnp.float32
                 )
-            cs[q, i % 4, i // 4] = total.astype(jnp.bfloat16)
+            cs[q][i % 4, i // 4] = total.astype(jnp.bfloat16)
             return carry
 
         lax.fori_loop(0, ROWS, per_row, 0)
 
     def update(q, last):
+        line, lo, width = CHUNKS[q]
+        part = slice(lo, lo + width)
+
         def per_pair(col, half, carry):
-            row = 4 * half + q
+            row = 4 * half + line
             flipped = lax.dot_general(
-                eye[...], fl[q, col, half], (((1,), (1,)), ((), ())),
+                eye[:width, :width], fl[q][col, half], (((1,), (1,)), ((), ())),
                 preferred_element_type=jnp.float32,
             )
+            if col < WHOLE:
+                own = cs[col][line, half, part, :]
+            else:
+                own = jnp.concatenate(
+                    [cs[k][line, half, part, :] for k in range(COUNT) if CHUNKS[k][0] == col],
+                    axis=1,
+                )
             total = (
-                k_v[row, col].astype(jnp.float32) + cs[col, q, half].astype(jnp.float32) + flipped
-            )
-            value = total / (vir[...] - occ[ig * ROWS + row] - occ[jg * CHUNKS + col])
+                k_v[row, col, part, :].astype(jnp.float32) + own.astype(jnp.float32) + flipped
+            )
+            value = total / (vir[part, :] - occ[ig * ROWS + row] - occ[jg * COLS + col])
             if last:
-                stage[q, half, col] = value
+                out_v[row, col, part, :] = value
             else:
-                t_v[col][row] = value.astype(jnp.bfloat16)
+                t_v[col][row, part, :] = value.astype(jnp.bfloat16)
             return carry
 
-        for col in range(CHUNKS):
+        for col in range(COLS):
             lax.fori_loop(0, 2, functools.partial(per_pair, col), 0)
-        if last:
-            for half in range(2):
-                out_copy(q, half).start()
-
-    def out_copy(q, half):
-        return pltpu.make_async_copy(
-            stage.at[q, half], out_h.at[4 * half + q], out_sem.at[q, half]
-        )
 
     def release(index, devices):
         for device in devices:
@@ -268,21 +288,23 @@
     vir[...] = across + across.T
     lax.fori_loop(0, NX * NC, choose, 0)
     lax.fori_loop(0, ROWS * NNB, locate, 0)
-    for q in range(CHUNKS):
-        t_load[q].wait()
+    for load in t_load:
+        load.wait()
+    for q in range(COUNT):
         pack(q)
     pl.semaphore_wait(barrier, 18 - inside.astype(jnp.int32))
 
     for step in range(ITERS):
         first, last = step == 0, step == ITERS - 1
         if not first:
-            for q in range(CHUNKS):
+            for q in range(COUNT):
                 for copy in exchange(q):
                     copy.wait_send()
             pl.semaphore_wait(free.at[0], len(ORDER))
             pack(0)
-        for q in range(CHUNKS - 1):
-            if not first:
+        early = [name[0] for name in SCHEDULE].index("C")
+        for q in range(early):
+            if not first and q + 1 < COUNT:
                 pack(q + 1)
             for copy in exchange(q):
                 copy.start()
@@ -291,50 +313,51 @@
             k_load.start()
             w_load.wait()
         else:
-            for q in range(CHUNKS):
+            for q in range(early + 1, COUNT):
+                pack(q)
+            for q in range(COUNT):
                 settle(q)
             release(2, x_peers)
             release(3, y_peers)
             for dy in range(NY):
                 for h in range(2):
                     meet(dy, h, free.at[1])
-        for q in range(CHUNKS):
-            for copy in exchange(q):
-                copy.wait_recv()
-            compute(q)
-            if not first and q == 0:
-                pl.semaphore_wait(free.at[1], 8 - inside.astype(jnp.int32))
-            spread(q)
-            if q >= 1:
-                if not first and q == 1:
+        waiting = {"S", "F", "D", "U"}
+        for name in SCHEDULE[early:]:
+            kind, q = name[0], int(name[1:])
+            if kind == "E":
+                for copy in exchange(q):
+                    copy.start()
+            elif kind == "C":
+                for copy in exchange(q):
+                    copy.wait_recv()
+                compute(q)
+                if not first and "S" in waiting:
+                    pl.semaphore_wait(free.at[1], 8 - inside.astype(jnp.int32))
+                waiting.discard("S")
+                spread(q)
+                if not last and q == COUNT - 1:
+                    release(0, ring_peers)
+            elif kind == "F":
+                if not first and "F" in waiting:
                     pl.semaphore_wait(free.at[2], NX - 1)
-                forward(q - 1)
-            if q == 1:
-                for copy in exchange(CHUNKS - 1):
-                    copy.start()
-            if q == 2:
-                if first:
+                waiting.discard("F")
+                forward(q)
+            elif kind == "D":
+                if not first and "D" in waiting:
+                    pl.semaphore_wait(free.at[3], NY - 1)
+                waiting.discard("D")
+                deliver(q)
+            else:
+                if first and "U" in waiting:
                     k_load.wait()
-                else:
-                    pl.semaphore_wait(free.at[3], NY - 1)
-                deliver(0)
-        if not last:
-            release(0, ring_peers)
-        deliver(1)
-        finish(0, last)
-        forward(3)
-        deliver(2)
-        finish(1, last)
-        deliver(3)
-        finish(2, last)
-        finish(3, last)
-
-    for q in range(CHUNKS):
+                waiting.discard("U")
+                finish(q, last)
+
+    for q in range(COUNT):
         for copy in exchange(q):
             copy.wait_send()
         settle(q)
-        for half in range(2):
-            out_copy(q, half).wait()
 
 
 def body(t_start, integrals, weights, neighbours, eps_occ, eps_vir):
@@ -343,6 +366,11 @@
     smem = pl.BlockSpec(memory_space=pltpu.SMEM)
     anywhere = pl.BlockSpec(memory_space=pl.ANY)
     dma = pltpu.SemaphoreType.DMA
+
+    def relayed(number, width):
+        sent = pltpu.VMEM((number, NX * NC * CAP, 256, width), bf16)
+        return [sent] + [pltpu.VMEM((number, 4, 2, 256, width), bf16)] * 4
+
     listed = neighbours.T
     bits = jnp.where(
         (listed // ROWS)[:, :, None] == jnp.arange(NX * NC, dtype=jnp.int32),
@@ -352,37 +380,32 @@
     masks = lax.reduce(bits, jnp.int32(0), lax.bitwise_or, (0, 2))
     return pl.pallas_call(
         sweeps_kernel,
-        out_shape=jax.ShapeDtypeStruct((ROWS, CHUNKS) + block, jnp.float32),
+        out_shape=pltpu.VMEM((ROWS, COLS) + block, jnp.float32),
         in_specs=[smem] * 3 + [pl.BlockSpec(memory_space=pltpu.VMEM)] + [anywhere] * 3,
-        out_specs=anywhere,
-        scratch_shapes=[pltpu.VMEM((ROWS,) + block, bf16)] * CHUNKS
-        + [
-            pltpu.VMEM((ROWS, CHUNKS) + block, bf16),
-            pltpu.VMEM((ROWS, NNB) + block, bf16),
-            pltpu.VMEM((CHUNKS, NX * NC * CAP) + block, bf16),
-        ]
-        + [pltpu.VMEM((NX * NC * CAP,) + block, bf16)] * CHUNKS
-        + [pltpu.VMEM((CHUNKS, 4, 2) + block, bf16)] * 4
+        out_specs=pl.BlockSpec(memory_space=pltpu.VMEM),
+        scratch_shapes=[pltpu.VMEM((ROWS,) + block, bf16)] * COLS
+        + [pltpu.VMEM((ROWS, COLS) + block, bf16), pltpu.VMEM((ROWS, NNB) + block, bf16)]
+        + [pltpu.VMEM((NX * NC * CAP, 256, width), bf16) for _, _, width in CHUNKS]
+        + relayed(WHOLE, 256)
+        + relayed(COUNT - WHOLE, 128)
         + [
             pltpu.VMEM(block, bf16),
             pltpu.VMEM(block, jnp.float32),
-            pltpu.VMEM((CHUNKS, 2, 4) + block, jnp.float32),
             pltpu.SMEM((NX * NC * CAP,), jnp.int32),
             pltpu.SMEM((ROWS * NNB,), jnp.int32),
-            dma((CHUNKS + 2,)),
-            dma((CHUNKS, 8)),
-            dma((CHUNKS, 8)),
-            dma((CHUNKS, 4, 2)),
-            dma((CHUNKS, 4, 2)),
-            dma((CHUNKS, 4)),
-            dma((CHUNKS, 4)),
-            dma((CHUNKS, 4)),
-            dma((CHUNKS, 4)),
-            dma((CHUNKS, 2)),
+            dma((COLS + 2,)),
+            dma((COUNT, 8)),
+            dma((COUNT, 8)),
+            dma((COUNT, 4, 2)),
+            dma((COUNT, 4, 2)),
+            dma((COUNT, 4)),
+            dma((COUNT, 4)),
+            dma((COUNT, 4)),
+            dma((COUNT, 4)),
             pltpu.SemaphoreType.REGULAR((4,)),
         ],
         compiler_params=pltpu.CompilerParams(
-            collective_id=0, has_side_effects=True, vmem_limit_bytes=67043328
+            collective_id=0, has_side_effects=True, vmem_limit_bytes=52 * 2**20
         ),
         name="sweeps",
     )(masks, listed, eps_occ, eps_vir.reshape(1, 256), t_start, integrals, weights)

time: 335 us -> 321 us (0.958)
  Pallas kernels: 321 us -> 313 us
  local copies, waits for them, and re-layouts: 7.8 us -> 3.54 us
    pallas_call x1, Pallas kernels: 321 us -> 313 us  [body(): pl.pallas_call(sweeps_kernel, out_shape=pltpu.VMEM((ROWS, COLS) + block,...]
    unnamed x1, local copies, waits for them, and re-layouts: 7.65 us -> 3.4 us
where the time goes in v3:
time: 321 us; the launch traced here: 318 us
  Pallas kernels  313 us (98%)
  local copies, waits for them, and re-layouts  3.54 us (1%)
    pallas_call x1, Pallas kernels, body(): pl.pallas_call(sweeps_kernel, out_shape=pltpu.VMEM((ROWS, COLS) + block,...  313 us

profile of v3, /device:TPU:0, one launch (start us, length us, event | category | flops | bytes accessed | tf_op | source)
XLA Modules:
  0.0 317.8 jit_solution(14722222569916417195)
XLA Ops:
  0.0 0.7 add_select_fusion.1
  0.7 0.1 eq.18
  0.8 0.1 broadcast_in_dim.17
  0.8 0.8 select_reduce_fusion.masks
  1.7 312.8 %sweeps.1 = f32[8,4,256,256]{3,2,1,0:T(8,128)S(1)} custom-call(s32[8,8]{1,0:T(8,128)} %select_reduce_fusion.masks, s32[8,64]{1,0:T(8,128)} %bitcast.4, f32[64]{0:T(128)} %occ.1, f32[1,256]{1,0:T(1,128)} %bitcast.5, bf16[8,4,256,256]{3,2,1,0:T(8,128)(2,1)} %t_h.1, bf16[8,4,256,256]{3,2,1,0:T(8,128)(2,1)} %k_h.1, bf16[8,8,256,256]{3,2,1,0:T(8,128)(2,1)} %w_h.1), custom_call_target="tpu_custom_call" | custom-call | tf_op jit(solution)/shard_map/sweeps/pallas_call | solution.py:381
  314.4 3.4 %copy.8 = f32[8,4,256,256]{3,2,1,0:T(8,128)} copy(f32[8,4,256,256]{3,2,1,0:T(8,128)S(1)} %sweeps.1) | data formatting | bytes 16777216
